TPU v7x, 128 devices: a whole 4x4x4 slice. The times are simulated.
128 devices in a mesh: row: 8 (over x_hi, y), col: 16 (over z, x_lo, core).
Axes of the slice: x: 4 (x_hi: 2, x_lo: 2; x = x_hi * 2 + x_lo), y: 4, z: 4, core: 2. Of those that a mesh axis runs over, the one named last changes fastest.
Arguments:
- doubles: float32 [32, 32, 192, 192], P(None, None, 'row', 'col'), may hold values from -6 to 6
- cycle_inter: float32 [6144, 6144], P('row', 'col'), may hold values from -0.078125 to 0.078125
Outputs:
- cycle_term: float32 [6144, 6144], P('row', 'col')
All inputs are finite; a program needn't handle non-finite values.
Results may differ from a plain program's by a relative error of at most 0.00007.
Values sent between devices are 32-bit elements; how exact they have to be, the bound alone decides.
A program may use at most 192 MiB of HBM per device.

v0:
```python
import jax
import jax.numpy as jnp
from jax import lax
from jax.sharding import PartitionSpec as P

V = 192


def body(doubles, cycle_inter):
    moved = lax.all_to_all(
        lax.all_to_all(doubles, "row", split_axis=0, concat_axis=2, tiled=True),
        "col",
        split_axis=1,
        concat_axis=3,
        tiled=True,
    )
    kloc = moved.shape[0]
    jloc = moved.shape[1]
    local_panel = jnp.transpose(moved, (0, 2, 1, 3)).reshape(kloc * V, jloc * V)
    amp_panel = lax.all_gather(local_panel, "row", axis=0, tiled=True)
    return jnp.dot(
        lax.all_gather(cycle_inter, "col", axis=1, tiled=True),
        amp_panel,
        precision=lax.Precision.HIGHEST,
        preferred_element_type=jnp.float32,
    )


def solution(mesh):
    placed = (P(None, None, "row", "col"), P("row", "col"))
    return jax.shard_map(
        body, mesh=mesh, in_specs=placed, out_specs=P("row", "col"), check_vma=False
    )
```

profile of v0, /device:TPU:1, one launch (start us, length us, event | category | flops | bytes accessed | tf_op | source)
XLA Modules:
  0.0 342.0 jit_solution(5271880841259820000)
XLA Ops:
  6.5 0.0 all-gather.5.cloned.1.call-start
  6.5 4.2 %reshape.4 = f32[8,1,36864]{2,1,0:T(1,128)S(1)} reshape(f32[32,12,24,32]{3,2,1,0:T(8,128)} %bitcast.20) | data formatting | bytes 2359296
  10.7 24.7 %all_to_all.36 = f32[8,1,36864]{2,1,0:T(1,128)S(1)} all-to-all(f32[8,1,36864]{2,1,0:T(1,128)S(1)} %reshape.4), channel_id=1, replica_groups=mesh['row'=8,'col'=16] {'row'}, dimensions={0} | all-to-all | bytes 2359296 | tf_op jit(solution)/shard_map/all_to_all | solution.py:11
  35.4 0.5 broadcast
  35.9 3.4 %reduce = f32[8,36864]{1,0:T(8,128)S(1)} reduce(f32[8,1,36864]{2,1,0:T(1,128)S(1)} %all_to_all.36, f32[]{:T(128)} %broadcast), dimensions={1}, to_apply=%all_to_all.26.reduce_sub_computation | reduce | bytes 2359300 | tf_op jit(solution)/shard_map/all_to_all | solution.py:11
  39.4 3.8 %reshape.5 = f32[32,12,24,32]{3,2,1,0:T(8,128)} reshape(f32[8,36864]{1,0:T(8,128)S(1)} %reduce) | data formatting | bytes 2359296
  43.1 6.3 %copy.10 = f32[8,4,32,24,12]{3,0,2,4,1:T(8,128)} copy(f32[8,4,32,24,12]{2,3,4,1,0:T(8,128)} %bitcast.17) | data formatting | bytes 2359296 | tf_op jit(solution)/shard_map/all_to_all | solution.py:11
  49.4 4.2 %all_to_all.29 = f32[4,32,192,12]{2,1,3,0:T(8,128)S(1)} reshape(f32[4,32,8,24,12]{3,2,1,4,0:T(8,128)} %bitcast.16) | data formatting | bytes 2359296 | tf_op jit(solution)/shard_map/all_to_all | solution.py:11
  53.6 1.0 copy.11
  54.7 28.3 %all_to_all.37 = f32[4,32,192,12]{2,0,3,1:T(4,128)S(1)} all-to-all(f32[4,32,192,12]{2,0,3,1:T(4,128)S(1)} %copy.11), channel_id=1, replica_groups=mesh['row'=8,'col'=16] {'col'}, dimensions={1} | all-to-all | bytes 2359296 | tf_op jit(solution)/shard_map/all_to_all | solution.py:10
  83.0 1.2 copy.12
  84.2 1.0 copy.13
  85.2 2.3 reshape.3
  87.5 0.0 all-gather.5.cloned.1.call-update
  87.5 0.2 all-gather.3.cloned.1.call-start
  87.7 0.5 all-gather.3.cloned.1.call-update
  88.3 110.7 %all-gather.5.cloned.1.call-done = f32[6144,384]{1,0:T(8,128)} async-done(((f32[768,384]{1,0:T(8,128)}), f32[6144,384]{1,0:T(8,128)}) %all-gather.5.cloned.1.call-update) | async-done | bytes 9437200 | tf_op jit(solution)/shard_map/all_gather | solution.py:20
  198.9 102.2 %all-gather.3.cloned.1.call-done = f32[768,6144]{1,0:T(8,128)} async-done(((f32[768,384]{1,0:T(8,128)}), f32[768,6144]{1,0:T(8,128)}) %all-gather.3.cloned.1.call-update) | async-done | bytes 18874384 | tf_op jit(solution)/shard_map/all_gather | solution.py:22
  301.1 34.1 %fusion = f32[768,384]{1,0:T(8,128)} fusion(f32[768,6144]{1,0:T(8,128)} %all-gather.3.cloned.1.call-done, f32[6144,384]{1,0:T(8,128)} %all-gather.5.cloned.1.call-done), kind=kOutput, calls=%fused_computation | convolution fusion | flops 21743271936 | bytes 29491200 | tf_op jit(solution)/shard_map/dot_general | solution.py:21
Async XLA Ops:
  6.5 192.4 %all-gather.5.cloned.1.call-start = ((), (), s32[]{:S(2)}) async-start(), calls=%async_computation.3 | async-start | bytes 10616832 | tf_op jit(solution)/shard_map/all_gather | solution.py:20
  87.5 213.6 %all-gather.3.cloned.1.call-start = ((), (), s32[]{:S(2)}) async-start(), calls=%async_computation.2 | async-start | bytes 20054016 | tf_op jit(solution)/shard_map/all_gather | solution.py:22
Sparse Core Ops, SparseCore 0:
  87.6 111.2 all-gather.4
  200.6 100.5 all-gather.2
where the time goes:
time: 342 us
  waiting for transfers between devices  213 us (62%)
  blocking collectives  53 us (15%)
  matrix products  34.1 us (10%)
  local copies, waits for them, and re-layouts  24.5 us (7%)
  between operations  13.4 us (4%)
  other arithmetic  3.45 us (1%)
    all_gather x1, waiting for transfers between devices, body(): amp_panel = lax.all_gather(local_panel, 'row', axis=0, tiled=True)  111 us
    all_gather x1, waiting for transfers between devices, body(): lax.all_gather(cycle_inter, 'col', axis=1, tiled=True)  102 us
    dot_general x1, matrix products, body(): jnp.dot(lax.all_gather(cycle_inter, 'col', axis=1, tiled=True), amp_panel...  34.1 us
    all_to_all x1, blocking collectives, body(): lax.all_to_all(lax.all_to_all(doubles, 'row', split_axis=0, concat_axis=2...  28.3 us
    all_to_all x1, blocking collectives, body(): lax.all_to_all(doubles, 'row', split_axis=0, concat_axis=2, tiled=True)  24.7 us
    all_to_all x4, local copies, waits for them, and re-layouts, body(): lax.all_to_all(doubles, 'row', split_axis=0, concat_axis=2, tiled=True)  12 us
    unnamed x2, local copies, waits for them, and re-layouts  7.95 us
  transfers between devices with their start and end apart: 2, of which 2 were waited for; matrix products, arithmetic and copies ran while one was open for 0% of the time, Pallas kernels for 0%

commit v1 on v0

--- a/solution.py
+++ b/solution.py
@@ -17,7 +17,9 @@
     kloc = moved.shape[0]
     jloc = moved.shape[1]
     local_panel = jnp.transpose(moved, (0, 2, 1, 3)).reshape(kloc * V, jloc * V)
-    amp_panel = lax.all_gather(local_panel, "row", axis=0, tiled=True)
+    amp_panel = jnp.concatenate(
+        lax.all_to_all(jnp.stack([local_panel] * lax.axis_size("row")), "row", 0, 0), axis=0
+    )
     return jnp.dot(
         lax.all_gather(cycle_inter, "col", axis=1, tiled=True),
         amp_panel,

time: 342 us -> 285 us (0.83)
  waiting for transfers between devices: 213 us -> 0.71 us
  blocking collectives: 53 us -> 208 us
    all_to_all x0 -> x1, blocking collectives: none -> 126 us  [body(): lax.all_to_all(jnp.stack([local_panel] * lax.axis_size('row')), 'row', 0, 0)]
    all_gather x1 -> x0, waiting for transfers between devices: 111 us -> none  [body(): amp_panel = lax.all_gather(local_panel, 'row', axis=0, tiled=True)]
    all_gather x1, waiting for transfers between devices: 102 us -> 0.01 us  [body(): lax.all_gather(cycle_inter, 'col', axis=1, tiled=True)]
    all_to_all x1, blocking collectives: 28.3 us -> 49.3 us  [body(): lax.all_to_all(lax.all_to_all(doubles, 'row', split_axis=0, concat_axis=2...]
    all_to_all x1, blocking collectives: 24.7 us -> 33.5 us  [body(): lax.all_to_all(doubles, 'row', split_axis=0, concat_axis=2, tiled=True)]
  transfers between devices with their start and end apart: 2 -> 1, of which waited for: 2 -> 0; matrix products, arithmetic and copies ran while one was open for 0% -> 8% of each run, Pallas kernels for 0% -> 0%
where the time goes in v1:
time: 285 us; the launch traced here: 284 us
  blocking collectives  208 us (73%)
  matrix products  34.1 us (12%)
  local copies, waits for them, and re-layouts  24.1 us (8%)
  between operations  13.5 us (5%)
  other arithmetic  3.45 us (1%)
    all_to_all x1, blocking collectives, body(): lax.all_to_all(jnp.stack([local_panel] * lax.axis_size('row')), 'row', 0, 0)  126 us
    all_to_all x1, blocking collectives, body(): lax.all_to_all(lax.all_to_all(doubles, 'row', split_axis=0, concat_axis=2...  49.3 us
    dot_general x1, matrix products, body(): jnp.dot(lax.all_gather(cycle_inter, 'col', axis=1, tiled=True), amp_panel...  34.1 us
    all_to_all x1, blocking collectives, body(): lax.all_to_all(doubles, 'row', split_axis=0, concat_axis=2, tiled=True)  33.5 us
    all_to_all x4, local copies, waits for them, and re-layouts, body(): lax.all_to_all(doubles, 'row', split_axis=0, concat_axis=2, tiled=True)  12.1 us
    unnamed x2, local copies, waits for them, and re-layouts  7.9 us
  transfers between devices with their start and end apart: 1, of which 0 were waited for; matrix products, arithmetic and copies ran while one was open for 8% of the time, Pallas kernels for 0%

profile of v1, /device:TPU:1, one launch (start us, length us, event | category | flops | bytes accessed | tf_op | source)
XLA Modules:
  0.0 284.3 jit_solution(9649727443030879012)
XLA Ops:
  6.5 0.0 all-gather.2.cloned.1.call-start
  6.5 0.7 all-gather.2.cloned.1.call-update
  7.3 4.2 %reshape.6 = f32[8,1,36864]{2,1,0:T(1,128)S(1)} reshape(f32[32,12,24,32]{3,2,1,0:T(8,128)} %bitcast.22) | data formatting | bytes 2359296
  11.5 33.5 %all_to_all.41 = f32[8,1,36864]{2,1,0:T(1,128)S(1)} all-to-all(f32[8,1,36864]{2,1,0:T(1,128)S(1)} %reshape.6), channel_id=1, replica_groups=mesh['row'=8,'col'=16] {'row'}, dimensions={0} | all-to-all | bytes 2359296 | tf_op jit(solution)/shard_map/all_to_all | solution.py:11
  45.0 0.5 broadcast.1
  45.5 3.4 %reduce = f32[8,36864]{1,0:T(8,128)S(1)} reduce(f32[8,1,36864]{2,1,0:T(1,128)S(1)} %all_to_all.41, f32[]{:T(128)} %broadcast.1), dimensions={1}, to_apply=%all_to_all.29.reduce_sub_computation | reduce | bytes 2359300 | tf_op jit(solution)/shard_map/all_to_all | solution.py:11
  49.0 3.7 %reshape.7 = f32[32,12,24,32]{3,2,1,0:T(8,128)} reshape(f32[8,36864]{1,0:T(8,128)S(1)} %reduce) | data formatting | bytes 2359296
  52.7 6.3 %copy.10 = f32[8,4,32,24,12]{3,0,2,4,1:T(8,128)} copy(f32[8,4,32,24,12]{2,3,4,1,0:T(8,128)} %bitcast.19) | data formatting | bytes 2359296 | tf_op jit(solution)/shard_map/all_to_all | solution.py:11
  59.0 4.3 %all_to_all.32 = f32[4,32,192,12]{2,1,3,0:T(8,128)S(1)} reshape(f32[4,32,8,24,12]{3,2,1,4,0:T(8,128)} %bitcast.18) | data formatting | bytes 2359296 | tf_op jit(solution)/shard_map/all_to_all | solution.py:11
  63.3 1.0 copy.11
  64.3 49.3 %all_to_all.42 = f32[4,32,192,12]{2,0,3,1:T(4,128)S(1)} all-to-all(f32[4,32,192,12]{2,0,3,1:T(4,128)S(1)} %copy.11), channel_id=1, replica_groups=mesh['row'=8,'col'=16] {'col'}, dimensions={1} | all-to-all | bytes 2359296 | tf_op jit(solution)/shard_map/all_to_all | solution.py:10
  113.7 1.2 copy.12
  114.9 1.0 copy.13
  115.9 1.2 stack_reshape.2
  117.1 0.6 stack.3
  117.8 125.6 %all_to_all.43 = f32[8,768,384]{2,1,0:T(8,128)} all-to-all(f32[8,768,384]{2,1,0:T(8,128)S(1)} %stack.3), channel_id=1, replica_groups=mesh['row'=8,'col'=16] {'row'}, dimensions={0} | all-to-all | bytes 18874368 | tf_op jit(solution)/shard_map/all_to_all | solution.py:21
  243.4 0.0 all-gather.2.cloned.1.call-done
  243.4 34.1 %fusion = f32[768,384]{1,0:T(8,128)} fusion(f32[768,6144]{1,0:T(8,128)} %all-gather.2.cloned.1.call-done, f32[6144,384]{1,0:T(8,128)} %bitcast.17), kind=kOutput, calls=%fused_computation | convolution fusion | flops 21743271936 | bytes 29491200 | tf_op jit(solution)/shard_map/dot_general | solution.py:23
Async XLA Ops:
  6.5 236.8 %all-gather.2.cloned.1.call-start = ((), (), s32[]{:S(2)}) async-start(), calls=%async_computation.3 | async-start | bytes 20054016 | tf_op jit(solution)/shard_map/all_gather | solution.py:24
Sparse Core Ops, SparseCore 0:
  9.0 148.4 all-gather.1

commit v2 on v0

--- a/solution.py
+++ b/solution.py
@@ -19,7 +19,7 @@
     local_panel = jnp.transpose(moved, (0, 2, 1, 3)).reshape(kloc * V, jloc * V)
     amp_panel = lax.all_gather(local_panel, "row", axis=0, tiled=True)
     return jnp.dot(
-        lax.all_gather(cycle_inter, "col", axis=1, tiled=True),
+        jnp.concatenate(lax.all_gather(cycle_inter, "col"), axis=1),
         amp_panel,
         precision=lax.Precision.HIGHEST,
         preferred_element_type=jnp.float32,

time: 342 us -> 302 us (0.88)
  waiting for transfers between devices: 213 us -> 124 us
  blocking collectives: 53 us -> 82.9 us
  local copies, waits for them, and re-layouts: 24.5 us -> 43.4 us
    all_gather x1, waiting for transfers between devices: 102 us -> 22.1 us  [body(): lax.all_gather(cycle_inter, 'col')]
    all_to_all x1, blocking collectives: 28.3 us -> 49.3 us  [body(): lax.all_to_all(lax.all_to_all(doubles, 'row', split_axis=0, concat_axis=2...]
    reshape x0 -> x1, local copies, waits for them, and re-layouts: none -> 18.9 us  [body(): jnp.concatenate(lax.all_gather(cycle_inter, 'col'), axis=1)]
    all_gather x1, waiting for transfers between devices: 111 us -> 101 us  [body(): amp_panel = lax.all_gather(local_panel, 'row', axis=0, tiled=True)]
    all_to_all x1, blocking collectives: 24.7 us -> 33.5 us  [body(): lax.all_to_all(doubles, 'row', split_axis=0, concat_axis=2, tiled=True)]
  transfers between devices with their start and end apart: 2 -> 2, of which waited for: 2 -> 2; matrix products, arithmetic and copies ran while one was open for 0% -> 14% of each run, Pallas kernels for 0% -> 0%
where the time goes in v2:
time: 302 us
  waiting for transfers between devices  124 us (41%)
  blocking collectives  82.9 us (27%)
  local copies, waits for them, and re-layouts  43.4 us (14%)
  matrix products  34.1 us (11%)
  between operations  13.4 us (4%)
  other arithmetic  3.45 us (1%)
    all_gather x1, waiting for transfers between devices, body(): amp_panel = lax.all_gather(local_panel, 'row', axis=0, tiled=True)  101 us
    all_to_all x1, blocking collectives, body(): lax.all_to_all(lax.all_to_all(doubles, 'row', split_axis=0, concat_axis=2...  49.3 us
    dot_general x1, matrix products, body(): jnp.dot(jnp.concatenate(lax.all_gather(cycle_inter, 'col'), axis=1), amp_...  34.1 us
    all_to_all x1, blocking collectives, body(): lax.all_to_all(doubles, 'row', split_axis=0, concat_axis=2, tiled=True)  33.5 us
    all_gather x1, waiting for transfers between devices, body(): lax.all_gather(cycle_inter, 'col')  22.1 us
    reshape x1, local copies, waits for them, and re-layouts, body(): jnp.concatenate(lax.all_gather(cycle_inter, 'col'), axis=1)  18.9 us
    all_to_all x4, local copies, waits for them, and re-layouts, body(): lax.all_to_all(doubles, 'row', split_axis=0, concat_axis=2, tiled=True)  12.1 us
    unnamed x2, local copies, waits for them, and re-layouts  7.91 us
  transfers between devices with their start and end apart: 2, of which 2 were waited for; matrix products, arithmetic and copies ran while one was open for 14% of the time, Pallas kernels for 0%

profile of v2, /device:TPU:1, one launch (start us, length us, event | category | flops | bytes accessed | tf_op | source)
XLA Modules:
  0.0 301.6 jit_solution(9303891821364243335)
XLA Ops:
  6.5 0.0 all-gather.6.cloned.1.call-start
  6.5 0.7 all-gather.6.cloned.1.call-update
  7.3 0.0 all-gather.4.cloned.1.call-start
  7.3 4.2 %reshape.13 = f32[8,1,36864]{2,1,0:T(1,128)S(1)} reshape(f32[32,12,24,32]{3,2,1,0:T(8,128)} %bitcast.26) | data formatting | bytes 2359296
  11.5 33.5 %all_to_all.36 = f32[8,1,36864]{2,1,0:T(1,128)S(1)} all-to-all(f32[8,1,36864]{2,1,0:T(1,128)S(1)} %reshape.13), channel_id=1, replica_groups=mesh['row'=8,'col'=16] {'row'}, dimensions={0} | all-to-all | bytes 2359296 | tf_op jit(solution)/shard_map/all_to_all | solution.py:11
  45.0 0.5 broadcast
  45.6 3.4 %reduce = f32[8,36864]{1,0:T(8,128)S(1)} reduce(f32[8,1,36864]{2,1,0:T(1,128)S(1)} %all_to_all.36, f32[]{:T(128)} %broadcast), dimensions={1}, to_apply=%all_to_all.26.reduce_sub_computation | reduce | bytes 2359300 | tf_op jit(solution)/shard_map/all_to_all | solution.py:11
  49.0 3.7 %reshape.14 = f32[32,12,24,32]{3,2,1,0:T(8,128)} reshape(f32[8,36864]{1,0:T(8,128)S(1)} %reduce) | data formatting | bytes 2359296
  52.7 6.3 %copy.16 = f32[8,4,32,24,12]{3,0,2,4,1:T(8,128)} copy(f32[8,4,32,24,12]{2,3,4,1,0:T(8,128)} %bitcast.23) | data formatting | bytes 2359296 | tf_op jit(solution)/shard_map/all_to_all | solution.py:11
  59.1 4.3 %all_to_all.29 = f32[4,32,192,12]{2,1,3,0:T(8,128)S(1)} reshape(f32[4,32,8,24,12]{3,2,1,4,0:T(8,128)} %bitcast.21) | data formatting | bytes 2359296 | tf_op jit(solution)/shard_map/all_to_all | solution.py:11
  63.3 1.0 copy.17
  64.4 49.3 %all_to_all.37 = f32[4,32,192,12]{2,0,3,1:T(4,128)S(1)} all-to-all(f32[4,32,192,12]{2,0,3,1:T(4,128)S(1)} %copy.17), channel_id=1, replica_groups=mesh['row'=8,'col'=16] {'col'}, dimensions={1} | all-to-all | bytes 2359296 | tf_op jit(solution)/shard_map/all_to_all | solution.py:10
  113.7 1.2 copy.18
  114.9 1.0 copy.19
  115.9 2.3 reshape.11
  118.2 0.0 all-gather.4.cloned.1.call-update
  118.2 22.1 %all-gather.6.cloned.1.call-done = f32[12288,384]{1,0:T(8,128)} async-done(((f32[768,384]{1,0:T(8,128)}), f32[12288,384]{1,0:T(8,128)}) %all-gather.6.cloned.1.call-update) | async-done | bytes 18874384 | tf_op jit(solution)/shard_map/all_gather | solution.py:22
  140.3 18.9 %copy.15 = f32[768,16,384]{0,2,1:T(8,128)} copy(f32[768,16,384]{2,0,1:T(8,128)} %bitcast.22) | data formatting | bytes 37748736 | tf_op jit(solution)/shard_map/reshape | solution.py:22
  159.2 101.4 %all-gather.4.cloned.1.call-done = f32[6144,384]{1,0:T(8,128)} async-done(((f32[768,384]{1,0:T(8,128)}), f32[6144,384]{1,0:T(8,128)}) %all-gather.4.cloned.1.call-update) | async-done | bytes 9437200 | tf_op jit(solution)/shard_map/all_gather | solution.py:20
  260.6 34.1 %fusion = f32[768,384]{1,0:T(8,128)} fusion(f32[768,6144]{0,1:T(8,128)} %bitcast.20, f32[6144,384]{1,0:T(8,128)} %all-gather.4.cloned.1.call-done), kind=kOutput, calls=%fused_computation | convolution fusion | flops 21743271936 | bytes 29491200 | tf_op jit(solution)/shard_map/dot_general | solution.py:21
Async XLA Ops:
  6.5 133.8 %all-gather.6.cloned.1.call-start = ((), (), s32[]{:S(2)}) async-start(), calls=%async_computation.3 | async-start | bytes 20054016 | tf_op jit(solution)/shard_map/all_gather | solution.py:22
  7.3 253.4 %all-gather.4.cloned.1.call-start = ((), (), s32[]{:S(2)}) async-start(), calls=%async_computation.2 | async-start | bytes 10616832 | tf_op jit(solution)/shard_map/all_gather | solution.py:20
Sparse Core Ops, SparseCore 0:
  9.0 131.2 all-gather.5
  142.6 117.9 all-gather.3
